TPU v7x, 32 devices: a whole 2x2x4 slice. The times are simulated.
32 devices in a mesh: member: 2 (over y), vec: 4 (over x, core), band: 4 (over z).
Axes of the slice: x: 2, y: 2, z: 4, core: 2. Of those that a mesh axis runs over, the one named last changes fastest.
Arguments:
- vectors: float32 [32, 3, 16, 1440], P(('member', 'vec'), None, 'band'), parts along dimension 0, may hold values from -6 to 6
- flow: float32 [4, 16, 1440], P(None, 'band'), may hold values from -1 to 1
- band_cut: int32 [16], replicated, may hold values from 2 to 127
- order: int32 [4], replicated, may hold values from 0 to 3, each once
Outputs:
- basis: float32 [32, 3, 16, 1440], P(('member', 'vec'), None, 'band'), parts along dimension 0
- growth: float32 [32], P(('member', 'vec')), parts along dimension 0
There are 2 independent parts, one for each index of `member`. A program takes and returns all parts, laid end to end along the dimension named above; an argument that names none is the same for every part. Nothing has to cross between parts.
Inputs may be any that keep to these rules, and one draw needn't show every extreme that they name: `order`: each block number appears once.
All inputs are finite; a program needn't handle non-finite values.
Results may differ from a plain program's by a relative error of at most 0.0001.
Values sent between devices are 32-bit elements; how exact they have to be, the bound alone decides.
A program may use at most 64 MiB of HBM per device.

v0:
```python
import math
import jax
import jax.numpy as jnp
from jax import lax
from jax.sharding import PartitionSpec as P

KMAX = 128
CAP_DEV = 2
step_dt = 0.4
half_dt = 0.2
sixth_dt = 0.4 / 6.0


def extended(block, sides, width):
    for axis, dim in sides:
        count = lax.axis_size(axis)
        forward = [(i, i + 1) for i in range(count - 1)]
        backward = [(target, source) for source, target in forward]
        low = lax.ppermute(
            lax.slice_in_dim(block, block.shape[dim] - width, None, axis=dim), axis, forward
        )
        high = lax.ppermute(lax.slice_in_dim(block, 0, width, axis=dim), axis, backward)
        block = jnp.concatenate([low, block, high], axis=dim)
    return block


def broadcast(value, axis, source):
    kept = jnp.where(lax.axis_index(axis) == source, value, 0).astype(value.dtype)
    return lax.psum(kept, axis)


def tendency(z, coef):
    inner = z[:, :, 1:-1]
    dx = 0.5 * (jnp.roll(inner, -1, 3) - jnp.roll(inner, 1, 3))
    dy = 0.5 * (z[:, :, 2:] - z[:, :, :-2])
    speed_x = coef[0]
    speed_y = coef[1]
    depth = 1.0 + 0.5 * coef[2]
    rotation = 0.5 * coef[3]
    advect = -(speed_x * dx + speed_y * dy)
    t_height = advect[:, 0] - depth * (dx[:, 1] + dy[:, 2])
    t_zonal = advect[:, 1] - dx[:, 0] + rotation * inner[:, 2]
    t_merid = advect[:, 2] - dy[:, 0] - rotation * inner[:, 1]
    return jnp.stack([t_height, t_zonal, t_merid], 1)


def with_rows(state):
    return extended(state, (("band", 2),), 1)


def step_near(state, flow):
    k_one = tendency(with_rows(state), flow)
    k_two = tendency(with_rows(state + half_dt * k_one), flow)
    k_three = tendency(with_rows(state + half_dt * k_two), flow)
    k_four = tendency(with_rows(state + step_dt * k_three), flow)
    return state + sixth_dt * (k_one + 2.0 * k_two + 2.0 * k_three + k_four)


def mode_table(nlon, kmax):
    points = jnp.arange(nlon, dtype=jnp.int32)
    waves = jnp.arange(kmax, dtype=jnp.int32)
    phase = (waves[:, None] * points[None, :] % nlon).astype(jnp.float32) * (2.0 * math.pi / nlon)
    scale = jnp.where(waves == 0, math.sqrt(1.0 / nlon), math.sqrt(2.0 / nlon)).astype(jnp.float32)
    cosines = jnp.cos(phase) * scale[:, None]
    sines = jnp.sin(phase) * math.sqrt(2.0 / nlon)
    return jnp.concatenate([cosines, sines], 0)


def project(rows, cutoff, table, kmax):
    waves = jnp.arange(kmax, dtype=jnp.int32)
    wave_both = jnp.concatenate([waves, waves], 0)
    keep = (wave_both <= cutoff[..., None]).astype(jnp.float32)
    coeffs = jnp.einsum("...l,kl->...k", rows, table, precision=lax.Precision.HIGHEST)
    return jnp.einsum("...k,kl->...l", coeffs * keep, table, precision=lax.Precision.HIGHEST)


def polar_filter(state, band_cut, table):
    nband = lax.axis_size("band")
    me_band = lax.axis_index("band")
    lat_dev = state.shape[2]
    cap_rows = CAP_DEV * lat_dev
    north = me_band < CAP_DEV
    south = me_band >= nband - CAP_DEV
    start = jnp.where(north, me_band * lat_dev, cap_rows + (me_band - nband + CAP_DEV) * lat_dev)
    start = jnp.clip(start, 0, 2 * cap_rows - lat_dev)
    cutoff = lax.dynamic_slice_in_dim(band_cut, start, lat_dev)
    return lax.cond(
        north | south, lambda value: project(value, cutoff, table, KMAX), lambda value: value, state
    )


def on_device(vectors, flow, band_cut, order):
    state = vectors
    nband = lax.axis_size("band")
    lat_dev = state.shape[2]
    table = mode_table(state.shape[3], KMAX)
    for inner_step in range(2):
        state = step_near(state, flow)
    state = polar_filter(state, band_cut, table)
    nblocks = lax.axis_size("vec")
    me_vec = lax.axis_index("vec")
    vec_dev = state.shape[0]
    total = float(3 * nband * lat_dev * state.shape[3])
    flat = state.reshape(vec_dev, -1)
    numbers = jnp.arange(nblocks, dtype=jnp.int32)
    position = jnp.sum(jnp.where(order == me_vec, numbers, 0))
    growth = jnp.zeros((vec_dev,), jnp.float32)
    for turn in range(nblocks):
        panel = broadcast(flat, "vec", order[turn])
        gram = lax.psum(jnp.dot(panel, panel.T, precision=lax.Precision.HIGHEST), "band") / total
        lower = jnp.linalg.cholesky(gram)
        ortho = jax.scipy.linalg.solve_triangular(lower, panel, lower=True)
        coef = lax.psum(jnp.dot(flat, ortho.T, precision=lax.Precision.HIGHEST), "band") / total
        update = flat - jnp.dot(coef, ortho, precision=lax.Precision.HIGHEST)
        flat = jnp.where(position > turn, update, jnp.where(position == turn, ortho, flat))
        growth = jnp.where(position == turn, jnp.log(jnp.diagonal(lower)), growth)
    return (flat.reshape(state.shape), growth)


def solution(mesh):
    in_specs = (P(("member", "vec"), None, "band", None), P(None, "band", None), P(), P())
    out_specs = (P(("member", "vec"), None, "band", None), P(("member", "vec")))
    return jax.shard_map(
        on_device, mesh=mesh, in_specs=in_specs, out_specs=out_specs, check_vma=False
    )
```

profile of v0, /device:TPU:0, one launch (start us, length us, event | category | flops | bytes accessed | tf_op | source)
XLA Modules:
  0.0 348.0 jit_solution(16133141258340314673)
XLA Ops:
  7.2 1.9 fusion.110
  10.4 5.6 %collective-permute-start.1 = (f32[4,3,1,1440]{3,2,1,0:T(1,128)}, f32[4,3,1,1440]{3,2,1,0:T(1,128)S(1)}, u32[]{:S(2)}, u32[]{:S(2)}) collective-permute-start(f32[4,3,1,1440]{3,2,1,0:T(1,128)} %get-tuple-element.172), channel_id=1, source_target_pairs={{0,1},{1,2},{2,3},{4,5},{5,6},{6,7},{8,9},{9,10},{10,11},{12,13},{... | collective-permute-start | bytes 207368 | tf_op jit(solution)/shard_map/ppermute | solution.py:19
  16.0 2.0 fusion.108
  18.1 3.1 sine_multiply_fusion
  23.9 1.6 broadcast_multiply_fusion.15
  27.3 4.6 %collective-permute-start.3 = (f32[4,3,1,1440]{3,2,1,0:T(1,128)S(1)}, f32[4,3,1,1440]{3,2,1,0:T(1,128)S(1)}, u32[]{:S(2)}, u32[]{:S(2)}) collective-permute-start(f32[4,3,1,1440]{3,2,1,0:T(1,128)S(1)} %get-tuple-element.166), channel_id=1, source_target_pairs={{0,1},{1,2},{2,3},{4,5},{5,6},{6,7},{8,9},{9,10},{10,11},{12,13},{... | collective-permute-start | bytes 207368 | tf_op jit(solution)/shard_map/ppermute | solution.py:19
  32.3 1.6 collective-permute-done.3
  36.2 4.9 %collective-permute-start.5 = (f32[4,3,1,1440]{3,2,1,0:T(1,128)S(1)}, f32[4,3,1,1440]{3,2,1,0:T(1,128)S(1)}, u32[]{:S(2)}, u32[]{:S(2)}) collective-permute-start(f32[4,3,1,1440]{3,2,1,0:T(1,128)S(1)} %get-tuple-element.160), channel_id=1, source_target_pairs={{0,1},{1,2},{2,3},{4,5},{5,6},{6,7},{8,9},{9,10},{10,11},{12,13},{... | collective-permute-start | bytes 207368 | tf_op jit(solution)/shard_map/ppermute | solution.py:19
  41.5 1.6 collective-permute-done.5
  45.5 4.9 %collective-permute-start.7 = (f32[4,3,1,1440]{3,2,1,0:T(1,128)S(1)}, f32[4,3,1,1440]{3,2,1,0:T(1,128)S(1)}, u32[]{:S(2)}, u32[]{:S(2)}) collective-permute-start(f32[4,3,1,1440]{3,2,1,0:T(1,128)S(1)} %get-tuple-element.154), channel_id=1, source_target_pairs={{0,1},{1,2},{2,3},{4,5},{5,6},{6,7},{8,9},{9,10},{10,11},{12,13},{... | collective-permute-start | bytes 207368 | tf_op jit(solution)/shard_map/ppermute | solution.py:19
  50.8 1.6 collective-permute-done.7
  54.9 4.9 %collective-permute-start.9 = (f32[4,3,1,1440]{3,2,1,0:T(1,128)S(1)}, f32[4,3,1,1440]{3,2,1,0:T(1,128)S(1)}, u32[]{:S(2)}, u32[]{:S(2)}) collective-permute-start(f32[4,3,1,1440]{3,2,1,0:T(1,128)S(1)} %get-tuple-element.148), channel_id=1, source_target_pairs={{0,1},{1,2},{2,3},{4,5},{5,6},{6,7},{8,9},{9,10},{10,11},{12,13},{... | collective-permute-start | bytes 207368 | tf_op jit(solution)/shard_map/ppermute | solution.py:19
  60.2 1.6 collective-permute-done.9
  64.4 5.1 %collective-permute-start.11 = (f32[4,3,1,1440]{3,2,1,0:T(1,128)S(1)}, f32[4,3,1,1440]{3,2,1,0:T(1,128)S(1)}, u32[]{:S(2)}, u32[]{:S(2)}) collective-permute-start(f32[4,3,1,1440]{3,2,1,0:T(1,128)S(1)} %get-tuple-element.142), channel_id=1, source_target_pairs={{0,1},{1,2},{2,3},{4,5},{5,6},{6,7},{8,9},{9,10},{10,11},{12,13},{... | collective-permute-start | bytes 207368 | tf_op jit(solution)/shard_map/ppermute | solution.py:19
  69.7 1.6 collective-permute-done.11
  73.8 4.9 %collective-permute-start.13 = (f32[4,3,1,1440]{3,2,1,0:T(1,128)S(1)}, f32[4,3,1,1440]{3,2,1,0:T(1,128)S(1)}, u32[]{:S(2)}, u32[]{:S(2)}) collective-permute-start(f32[4,3,1,1440]{3,2,1,0:T(1,128)S(1)} %get-tuple-element.136), channel_id=1, source_target_pairs={{0,1},{1,2},{2,3},{4,5},{5,6},{6,7},{8,9},{9,10},{10,11},{12,13},{... | collective-permute-start | bytes 207368 | tf_op jit(solution)/shard_map/ppermute | solution.py:19
  79.1 1.6 collective-permute-done.13
  83.3 4.9 %collective-permute-start.15 = (f32[4,3,1,1440]{3,2,1,0:T(1,128)S(1)}, f32[4,3,1,1440]{3,2,1,0:T(1,128)S(1)}, u32[]{:S(2)}, u32[]{:S(2)}) collective-permute-start(f32[4,3,1,1440]{3,2,1,0:T(1,128)S(1)} %get-tuple-element.130), channel_id=1, source_target_pairs={{0,1},{1,2},{2,3},{4,5},{5,6},{6,7},{8,9},{9,10},{10,11},{12,13},{... | collective-permute-start | bytes 207368 | tf_op jit(solution)/shard_map/ppermute | solution.py:19
  88.6 1.6 collective-permute-done.15
  91.4 2.6 conditional.1
  92.7 1.4 fusion
  97.8 32.7 %all-reduce.5.cloned.1.call-done = f32[4,17280]{1,0:T(4,128)} async-done(((f32[4,17280]{1,0:T(4,128)}), f32[4,17280]{1,0:T(4,128)}) %all-reduce.5.cloned.1.call-update) | async-done | bytes 276496 | tf_op jit(solution)/shard_map/psum | solution.py:29
  130.6 2.3 fusion.112
  132.9 11.7 %psum.85 = f32[4,4]{0,1:T(4,128)S(1)} all-reduce(f32[4,4]{0,1:T(4,128)S(1)} %fusion.112), channel_id=1, replica_groups=mesh['member'=2,'vec'=4,'band'=4] {'band'}, use_global_device_ids=true, to_apply=%region_4.5 | all-reduce | flops 16 | bytes 128 | tf_op jit(solution)/shard_map/psum | solution.py:110
  146.7 1.7 fusion.66
  148.4 1.3 fusion.113
  149.7 8.4 %psum.86 = f32[4,4]{0,1:T(4,128)S(1)} all-reduce(f32[4,4]{0,1:T(4,128)S(1)} %fusion.113), channel_id=1, replica_groups=mesh['member'=2,'vec'=4,'band'=4] {'band'}, use_global_device_ids=true, to_apply=%region_7.10 | all-reduce | flops 16 | bytes 128 | tf_op jit(solution)/shard_map/psum | solution.py:113
  158.1 1.5 broadcast_select_fusion.2
  161.5 29.0 %all-reduce.7.cloned.1.call-done = f32[4,17280]{1,0:T(4,128)} async-done(((f32[4,17280]{1,0:T(4,128)}), f32[4,17280]{1,0:T(4,128)}) %all-reduce.7.cloned.1.call-update) | async-done | bytes 276496 | tf_op jit(solution)/shard_map/psum | solution.py:29
  190.6 2.3 fusion.114
  192.9 11.9 %psum.88 = f32[4,4]{0,1:T(4,128)S(1)} all-reduce(f32[4,4]{0,1:T(4,128)S(1)} %fusion.114), channel_id=1, replica_groups=mesh['member'=2,'vec'=4,'band'=4] {'band'}, use_global_device_ids=true, to_apply=%region_9.12 | all-reduce | flops 16 | bytes 128 | tf_op jit(solution)/shard_map/psum | solution.py:110
  207.0 1.7 fusion.64
  208.7 1.3 fusion.115
  210.0 8.4 %psum.89 = f32[4,4]{0,1:T(4,128)S(1)} all-reduce(f32[4,4]{0,1:T(4,128)S(1)} %fusion.115), channel_id=1, replica_groups=mesh['member'=2,'vec'=4,'band'=4] {'band'}, use_global_device_ids=true, to_apply=%region_10.13 | all-reduce | flops 16 | bytes 128 | tf_op jit(solution)/shard_map/psum | solution.py:113
  218.3 1.5 broadcast_select_fusion.1
  221.8 29.0 %all-reduce.9.cloned.1.call-done = f32[4,17280]{1,0:T(4,128)} async-done(((f32[4,17280]{1,0:T(4,128)}), f32[4,17280]{1,0:T(4,128)}) %all-reduce.9.cloned.1.call-update) | async-done | bytes 276496 | tf_op jit(solution)/shard_map/psum | solution.py:29
  250.8 2.3 fusion.116
  253.2 11.7 %psum.91 = f32[4,4]{0,1:T(4,128)S(1)} all-reduce(f32[4,4]{0,1:T(4,128)S(1)} %fusion.116), channel_id=1, replica_groups=mesh['member'=2,'vec'=4,'band'=4] {'band'}, use_global_device_ids=true, to_apply=%region_12.15 | all-reduce | flops 16 | bytes 128 | tf_op jit(solution)/shard_map/psum | solution.py:110
  267.0 1.7 fusion.62
  268.7 1.3 fusion.117
  270.0 8.4 %psum.92 = f32[4,4]{0,1:T(4,128)S(1)} all-reduce(f32[4,4]{0,1:T(4,128)S(1)} %fusion.117), channel_id=1, replica_groups=mesh['member'=2,'vec'=4,'band'=4] {'band'}, use_global_device_ids=true, to_apply=%region_13.16 | all-reduce | flops 16 | bytes 128 | tf_op jit(solution)/shard_map/psum | solution.py:113
  278.4 1.5 broadcast_select_fusion
  283.1 27.8 %all-reduce.11.cloned.1.call-done = f32[4,17280]{1,0:T(4,128)} async-done(((f32[4,17280]{1,0:T(4,128)}), f32[4,17280]{1,0:T(4,128)}) %all-reduce.11.cloned.1.call-update) | async-done | bytes 276496 | tf_op jit(solution)/shard_map/psum | solution.py:29
  310.9 2.3 fusion.118
  313.3 11.7 %psum.94 = f32[4,4]{0,1:T(4,128)S(1)} all-reduce(f32[4,4]{0,1:T(4,128)S(1)} %fusion.118), channel_id=1, replica_groups=mesh['member'=2,'vec'=4,'band'=4] {'band'}, use_global_device_ids=true, to_apply=%region_15.18 | all-reduce | flops 16 | bytes 128 | tf_op jit(solution)/shard_map/psum | solution.py:110
  327.7 1.7 fusion.60
  329.4 1.3 fusion.119
  330.7 8.4 %psum.95 = f32[4,4]{0,1:T(4,128)S(1)} all-reduce(f32[4,4]{0,1:T(4,128)S(1)} %fusion.119), channel_id=1, replica_groups=mesh['member'=2,'vec'=4,'band'=4] {'band'}, use_global_device_ids=true, to_apply=%region_16.19 | all-reduce | flops 16 | bytes 128 | tf_op jit(solution)/shard_map/psum | solution.py:113
  (134 shorter events, 40.6 us)
Async XLA Ops:
  7.2 10.8 %copy-start = (f32[4,3,4,1440]{3,2,1,0:T(4,128)S(1)}, f32[4,3,4,1440]{3,2,1,0:T(4,128)}, u32[]{:S(2)}) copy-start(f32[4,3,4,1440]{3,2,1,0:T(4,128)} %param.9) | copy-start | bytes 829444
  7.2 10.9 %copy-start.1 = (f32[4,4,1440]{2,1,0:T(4,128)S(1)}, f32[4,4,1440]{2,1,0:T(4,128)}, u32[]{:S(2)}) copy-start(f32[4,4,1440]{2,1,0:T(4,128)} %param.10) | copy-start | bytes 276484
  7.2 123.4 %all-reduce.5.cloned.1.call-start = ((), (), s32[]{:S(2)}) async-start(), calls=%async_computation | async-start | bytes 552960 | tf_op jit(solution)/shard_map/psum | solution.py:29
  9.1 14.1 %collective-permute-start = (f32[4,3,1,1440]{3,2,1,0:T(1,128)}, f32[4,3,1,1440]{3,2,1,0:T(1,128)S(1)}, u32[]{:S(2)}, u32[]{:S(2)}) collective-permute-start(f32[4,3,1,1440]{3,2,1,0:T(1,128)} %get-tuple-element.171), channel_id=1, source_target_pairs={{1,0},{2,1},{3,2},{5,4},{6,5},{7,6},{9,8},{10,9},{11,10},{13,12},{... | collective-permute-start | bytes 207368 | tf_op jit(solution)/shard_map/ppermute | solution.py:22
  10.4 12.8 %collective-permute-start.1 = (f32[4,3,1,1440]{3,2,1,0:T(1,128)}, f32[4,3,1,1440]{3,2,1,0:T(1,128)S(1)}, u32[]{:S(2)}, u32[]{:S(2)}) collective-permute-start(f32[4,3,1,1440]{3,2,1,0:T(1,128)} %get-tuple-element.172), channel_id=1, source_target_pairs={{0,1},{1,2},{2,3},{4,5},{5,6},{6,7},{8,9},{9,10},{10,11},{12,13},{... | collective-permute-start | bytes 207368 | tf_op jit(solution)/shard_map/ppermute | solution.py:19
  21.2 0.7 copy-start.4
  23.2 0.6 copy-start.2
  23.2 0.6 copy-start.3
  26.0 6.2 %collective-permute-start.2 = (f32[4,3,1,1440]{3,2,1,0:T(1,128)S(1)}, f32[4,3,1,1440]{3,2,1,0:T(1,128)S(1)}, u32[]{:S(2)}, u32[]{:S(2)}) collective-permute-start(f32[4,3,1,1440]{3,2,1,0:T(1,128)S(1)} %get-tuple-element.165), channel_id=1, source_target_pairs={{1,0},{2,1},{3,2},{5,4},{6,5},{7,6},{9,8},{10,9},{11,10},{13,12},{... | collective-permute-start | bytes 207368 | tf_op jit(solution)/shard_map/ppermute | solution.py:22
  27.3 6.5 %collective-permute-start.3 = (f32[4,3,1,1440]{3,2,1,0:T(1,128)S(1)}, f32[4,3,1,1440]{3,2,1,0:T(1,128)S(1)}, u32[]{:S(2)}, u32[]{:S(2)}) collective-permute-start(f32[4,3,1,1440]{3,2,1,0:T(1,128)S(1)} %get-tuple-element.166), channel_id=1, source_target_pairs={{0,1},{1,2},{2,3},{4,5},{5,6},{6,7},{8,9},{9,10},{10,11},{12,13},{... | collective-permute-start | bytes 207368 | tf_op jit(solution)/shard_map/ppermute | solution.py:19
  34.9 6.6 %collective-permute-start.4 = (f32[4,3,1,1440]{3,2,1,0:T(1,128)S(1)}, f32[4,3,1,1440]{3,2,1,0:T(1,128)S(1)}, u32[]{:S(2)}, u32[]{:S(2)}) collective-permute-start(f32[4,3,1,1440]{3,2,1,0:T(1,128)S(1)} %get-tuple-element.159), channel_id=1, source_target_pairs={{1,0},{2,1},{3,2},{5,4},{6,5},{7,6},{9,8},{10,9},{11,10},{13,12},{... | collective-permute-start | bytes 207368 | tf_op jit(solution)/shard_map/ppermute | solution.py:22
  36.2 6.9 %collective-permute-start.5 = (f32[4,3,1,1440]{3,2,1,0:T(1,128)S(1)}, f32[4,3,1,1440]{3,2,1,0:T(1,128)S(1)}, u32[]{:S(2)}, u32[]{:S(2)}) collective-permute-start(f32[4,3,1,1440]{3,2,1,0:T(1,128)S(1)} %get-tuple-element.160), channel_id=1, source_target_pairs={{0,1},{1,2},{2,3},{4,5},{5,6},{6,7},{8,9},{9,10},{10,11},{12,13},{... | collective-permute-start | bytes 207368 | tf_op jit(solution)/shard_map/ppermute | solution.py:19
  44.2 6.6 %collective-permute-start.6 = (f32[4,3,1,1440]{3,2,1,0:T(1,128)S(1)}, f32[4,3,1,1440]{3,2,1,0:T(1,128)S(1)}, u32[]{:S(2)}, u32[]{:S(2)}) collective-permute-start(f32[4,3,1,1440]{3,2,1,0:T(1,128)S(1)} %get-tuple-element.153), channel_id=1, source_target_pairs={{1,0},{2,1},{3,2},{5,4},{6,5},{7,6},{9,8},{10,9},{11,10},{13,12},{... | collective-permute-start | bytes 207368 | tf_op jit(solution)/shard_map/ppermute | solution.py:22
  45.5 6.9 %collective-permute-start.7 = (f32[4,3,1,1440]{3,2,1,0:T(1,128)S(1)}, f32[4,3,1,1440]{3,2,1,0:T(1,128)S(1)}, u32[]{:S(2)}, u32[]{:S(2)}) collective-permute-start(f32[4,3,1,1440]{3,2,1,0:T(1,128)S(1)} %get-tuple-element.154), channel_id=1, source_target_pairs={{0,1},{1,2},{2,3},{4,5},{5,6},{6,7},{8,9},{9,10},{10,11},{12,13},{... | collective-permute-start | bytes 207368 | tf_op jit(solution)/shard_map/ppermute | solution.py:19
  53.6 6.6 %collective-permute-start.8 = (f32[4,3,1,1440]{3,2,1,0:T(1,128)S(1)}, f32[4,3,1,1440]{3,2,1,0:T(1,128)S(1)}, u32[]{:S(2)}, u32[]{:S(2)}) collective-permute-start(f32[4,3,1,1440]{3,2,1,0:T(1,128)S(1)} %get-tuple-element.147), channel_id=1, source_target_pairs={{1,0},{2,1},{3,2},{5,4},{6,5},{7,6},{9,8},{10,9},{11,10},{13,12},{... | collective-permute-start | bytes 207368 | tf_op jit(solution)/shard_map/ppermute | solution.py:22
  54.9 6.9 %collective-permute-start.9 = (f32[4,3,1,1440]{3,2,1,0:T(1,128)S(1)}, f32[4,3,1,1440]{3,2,1,0:T(1,128)S(1)}, u32[]{:S(2)}, u32[]{:S(2)}) collective-permute-start(f32[4,3,1,1440]{3,2,1,0:T(1,128)S(1)} %get-tuple-element.148), channel_id=1, source_target_pairs={{0,1},{1,2},{2,3},{4,5},{5,6},{6,7},{8,9},{9,10},{10,11},{12,13},{... | collective-permute-start | bytes 207368 | tf_op jit(solution)/shard_map/ppermute | solution.py:19
  63.1 6.6 %collective-permute-start.10 = (f32[4,3,1,1440]{3,2,1,0:T(1,128)S(1)}, f32[4,3,1,1440]{3,2,1,0:T(1,128)S(1)}, u32[]{:S(2)}, u32[]{:S(2)}) collective-permute-start(f32[4,3,1,1440]{3,2,1,0:T(1,128)S(1)} %get-tuple-element.141), channel_id=1, source_target_pairs={{1,0},{2,1},{3,2},{5,4},{6,5},{7,6},{9,8},{10,9},{11,10},{13,12},{... | collective-permute-start | bytes 207368 | tf_op jit(solution)/shard_map/ppermute | solution.py:22
  64.4 6.9 %collective-permute-start.11 = (f32[4,3,1,1440]{3,2,1,0:T(1,128)S(1)}, f32[4,3,1,1440]{3,2,1,0:T(1,128)S(1)}, u32[]{:S(2)}, u32[]{:S(2)}) collective-permute-start(f32[4,3,1,1440]{3,2,1,0:T(1,128)S(1)} %get-tuple-element.142), channel_id=1, source_target_pairs={{0,1},{1,2},{2,3},{4,5},{5,6},{6,7},{8,9},{9,10},{10,11},{12,13},{... | collective-permute-start | bytes 207368 | tf_op jit(solution)/shard_map/ppermute | solution.py:19
  72.5 6.6 %collective-permute-start.12 = (f32[4,3,1,1440]{3,2,1,0:T(1,128)S(1)}, f32[4,3,1,1440]{3,2,1,0:T(1,128)S(1)}, u32[]{:S(2)}, u32[]{:S(2)}) collective-permute-start(f32[4,3,1,1440]{3,2,1,0:T(1,128)S(1)} %get-tuple-element.135), channel_id=1, source_target_pairs={{1,0},{2,1},{3,2},{5,4},{6,5},{7,6},{9,8},{10,9},{11,10},{13,12},{... | collective-permute-start | bytes 207368 | tf_op jit(solution)/shard_map/ppermute | solution.py:22
  73.8 6.9 %collective-permute-start.13 = (f32[4,3,1,1440]{3,2,1,0:T(1,128)S(1)}, f32[4,3,1,1440]{3,2,1,0:T(1,128)S(1)}, u32[]{:S(2)}, u32[]{:S(2)}) collective-permute-start(f32[4,3,1,1440]{3,2,1,0:T(1,128)S(1)} %get-tuple-element.136), channel_id=1, source_target_pairs={{0,1},{1,2},{2,3},{4,5},{5,6},{6,7},{8,9},{9,10},{10,11},{12,13},{... | collective-permute-start | bytes 207368 | tf_op jit(solution)/shard_map/ppermute | solution.py:19
  82.0 6.6 %collective-permute-start.14 = (f32[4,3,1,1440]{3,2,1,0:T(1,128)S(1)}, f32[4,3,1,1440]{3,2,1,0:T(1,128)S(1)}, u32[]{:S(2)}, u32[]{:S(2)}) collective-permute-start(f32[4,3,1,1440]{3,2,1,0:T(1,128)S(1)} %get-tuple-element.129), channel_id=1, source_target_pairs={{1,0},{2,1},{3,2},{5,4},{6,5},{7,6},{9,8},{10,9},{11,10},{13,12},{... | collective-permute-start | bytes 207368 | tf_op jit(solution)/shard_map/ppermute | solution.py:22
  83.3 6.9 %collective-permute-start.15 = (f32[4,3,1,1440]{3,2,1,0:T(1,128)S(1)}, f32[4,3,1,1440]{3,2,1,0:T(1,128)S(1)}, u32[]{:S(2)}, u32[]{:S(2)}) collective-permute-start(f32[4,3,1,1440]{3,2,1,0:T(1,128)S(1)} %get-tuple-element.130), channel_id=1, source_target_pairs={{0,1},{1,2},{2,3},{4,5},{5,6},{6,7},{8,9},{9,10},{10,11},{12,13},{... | collective-permute-start | bytes 207368 | tf_op jit(solution)/shard_map/ppermute | solution.py:19
  90.8 0.7 copy-start.5
  95.2 95.4 %all-reduce.7.cloned.1.call-start = ((), (), s32[]{:S(2)}) async-start(), calls=%async_computation.1 | async-start | bytes 552960 | tf_op jit(solution)/shard_map/psum | solution.py:29
  159.6 91.2 %all-reduce.9.cloned.1.call-start = ((), (), s32[]{:S(2)}) async-start(), calls=%async_computation.2 | async-start | bytes 552960 | tf_op jit(solution)/shard_map/psum | solution.py:29
  219.9 91.0 %all-reduce.11.cloned.1.call-start = ((), (), s32[]{:S(2)}) async-start(), calls=%async_computation.3 | async-start | bytes 552960 | tf_op jit(solution)/shard_map/psum | solution.py:29
Sparse Core Ops, SparseCore 0:
  95.4 35.1 all-reduce.4
  159.7 30.8 all-reduce.6
  220.0 30.8 all-reduce.8
  280.1 30.8 all-reduce.10
where the time goes:
time: 349 us; the launch traced here: 348 us
  waiting for transfers between devices  132 us (38%)
  blocking collectives  80.3 us (23%)
  starting transfers between devices  50.2 us (14%)
  matrix products  29.2 us (8%)
  between operations  21.9 us (6%)
  other arithmetic  21.5 us (6%)
  local copies, waits for them, and re-layouts  13.3 us (4%)
    psum x4, waiting for transfers between devices, broadcast(): return lax.psum(kept, axis)  119 us
    psum x4, blocking collectives, on_device(): lax.psum(jnp.dot(panel, panel.T, precision=lax.Precision.HIGHEST), 'band')  46.9 us
    ppermute x8, starting transfers between devices, extended(): lax.ppermute(lax.slice_in_dim(block, block.shape[dim] - width, None, axis...  39.7 us
    psum x4, blocking collectives, on_device(): lax.psum(jnp.dot(flat, ortho.T, precision=lax.Precision.HIGHEST), 'band')  33.4 us
    ppermute x8, waiting for transfers between devices, extended(): lax.ppermute(lax.slice_in_dim(block, block.shape[dim] - width, None, axis...  11 us
    ppermute x8, starting transfers between devices, extended(): lax.ppermute(lax.slice_in_dim(block, 0, width, axis=dim), axis, backward)  10.3 us
    dot_general x4, matrix products, on_device(): jnp.dot(panel, panel.T, precision=lax.Precision.HIGHEST)  9.4 us
  transfers between devices with their start and end apart: 20, of which 18 were waited for; matrix products, arithmetic and copies ran while one was open for 3% of the time, Pallas kernels for 0%

commit v1 on v0

--- a/solution.py
+++ b/solution.py
@@ -26,7 +26,7 @@
 
 def broadcast(value, axis, source):
     kept = jnp.where(lax.axis_index(axis) == source, value, 0).astype(value.dtype)
-    return lax.psum(kept, axis)
+    return jnp.sum(lax.all_gather(kept, axis), axis=0)
 
 
 def tendency(z, coef):

time: 349 us -> 288 us (0.83)
  waiting for transfers between devices: 132 us -> 71.7 us
  matrix products: 29.2 us -> 18.9 us
  other arithmetic: 21.5 us -> 29.1 us
    psum x4 -> x0, waiting for transfers between devices: 119 us -> none  [broadcast(): return lax.psum(kept, axis)]
    all_gather x0 -> x4, waiting for transfers between devices: none -> 58.6 us  [broadcast(): return jnp.sum(lax.all_gather(kept, axis), axis=0)]
    reduce_sum x0 -> x4, other arithmetic: none -> 6.01 us  [broadcast(): return jnp.sum(lax.all_gather(kept, axis), axis=0)]
    dot_general x4, matrix products: 9.4 us -> 5.12 us  [on_device(): jnp.dot(panel, panel.T, precision=lax.Precision.HIGHEST)]
    another operation x4, matrix products: 6.71 us -> 2.91 us  [on_device(): ortho = jax.scipy.linalg.solve_triangular(lower, panel, lower=True)]
where the time goes in v1:
time: 288 us; the launch traced here: 287 us
  blocking collectives  80.4 us (28%)
  waiting for transfers between devices  71.7 us (25%)
  starting transfers between devices  50.2 us (17%)
  other arithmetic  29.1 us (10%)
  between operations  21.8 us (8%)
  matrix products  18.9 us (7%)
  local copies, waits for them, and re-layouts  14.4 us (5%)
    all_gather x4, waiting for transfers between devices, broadcast(): return jnp.sum(lax.all_gather(kept, axis), axis=0)  58.6 us
    psum x4, blocking collectives, on_device(): lax.psum(jnp.dot(panel, panel.T, precision=lax.Precision.HIGHEST), 'band')  46.9 us
    ppermute x8, starting transfers between devices, extended(): lax.ppermute(lax.slice_in_dim(block, block.shape[dim] - width, None, axis...  39.7 us
    psum x4, blocking collectives, on_device(): lax.psum(jnp.dot(flat, ortho.T, precision=lax.Precision.HIGHEST), 'band')  33.5 us
    ppermute x8, waiting for transfers between devices, extended(): lax.ppermute(lax.slice_in_dim(block, block.shape[dim] - width, None, axis...  11 us
    ppermute x8, starting transfers between devices, extended(): lax.ppermute(lax.slice_in_dim(block, 0, width, axis=dim), axis, backward)  10.3 us
    reduce_sum x4, other arithmetic, broadcast(): return jnp.sum(lax.all_gather(kept, axis), axis=0)  6.01 us
  transfers between devices with their start and end apart: 20, of which 18 were waited for; matrix products, arithmetic and copies ran while one was open for 3% of the time, Pallas kernels for 0%

profile of v1, /device:TPU:0, one launch (start us, length us, event | category | flops | bytes accessed | tf_op | source)
XLA Modules:
  0.0 286.6 jit_solution(21368821735371907)
XLA Ops:
  7.2 1.9 fusion.110
  10.4 5.6 %collective-permute-start.1 = (f32[4,3,1,1440]{3,2,1,0:T(1,128)}, f32[4,3,1,1440]{3,2,1,0:T(1,128)S(1)}, u32[]{:S(2)}, u32[]{:S(2)}) collective-permute-start(f32[4,3,1,1440]{3,2,1,0:T(1,128)} %get-tuple-element.203), channel_id=1, source_target_pairs={{0,1},{1,2},{2,3},{4,5},{5,6},{6,7},{8,9},{9,10},{10,11},{12,13},{... | collective-permute-start | bytes 207368 | tf_op jit(solution)/shard_map/ppermute | solution.py:19
  16.0 2.0 fusion.108
  18.1 3.1 %sine_multiply_fusion = (f32[128,1440]{0,1:T(8,128)S(1)}, f32[128,1440]{0,1:T(8,128)S(1)}) fusion(f32[128]{0:T(128)S(1)} %compare_select_fusion), kind=kLoop, calls=%fused_computation.23 | loop fusion | flops 2027520 | bytes 1475072 | tf_op jit(solution)/shard_map/mul | solution.py:65
  23.9 1.6 broadcast_multiply_fusion.15
  26.0 1.3 collective-permute-start.2
  27.3 4.6 %collective-permute-start.3 = (f32[4,3,1,1440]{3,2,1,0:T(1,128)S(1)}, f32[4,3,1,1440]{3,2,1,0:T(1,128)S(1)}, u32[]{:S(2)}, u32[]{:S(2)}) collective-permute-start(f32[4,3,1,1440]{3,2,1,0:T(1,128)S(1)} %get-tuple-element.197), channel_id=1, source_target_pairs={{0,1},{1,2},{2,3},{4,5},{5,6},{6,7},{8,9},{9,10},{10,11},{12,13},{... | collective-permute-start | bytes 207368 | tf_op jit(solution)/shard_map/ppermute | solution.py:19
  32.3 1.6 collective-permute-done.3
  34.9 1.3 collective-permute-start.4
  36.2 4.9 %collective-permute-start.5 = (f32[4,3,1,1440]{3,2,1,0:T(1,128)S(1)}, f32[4,3,1,1440]{3,2,1,0:T(1,128)S(1)}, u32[]{:S(2)}, u32[]{:S(2)}) collective-permute-start(f32[4,3,1,1440]{3,2,1,0:T(1,128)S(1)} %get-tuple-element.191), channel_id=1, source_target_pairs={{0,1},{1,2},{2,3},{4,5},{5,6},{6,7},{8,9},{9,10},{10,11},{12,13},{... | collective-permute-start | bytes 207368 | tf_op jit(solution)/shard_map/ppermute | solution.py:19
  41.5 1.6 collective-permute-done.5
  44.2 1.3 collective-permute-start.6
  45.5 4.9 %collective-permute-start.7 = (f32[4,3,1,1440]{3,2,1,0:T(1,128)S(1)}, f32[4,3,1,1440]{3,2,1,0:T(1,128)S(1)}, u32[]{:S(2)}, u32[]{:S(2)}) collective-permute-start(f32[4,3,1,1440]{3,2,1,0:T(1,128)S(1)} %get-tuple-element.185), channel_id=1, source_target_pairs={{0,1},{1,2},{2,3},{4,5},{5,6},{6,7},{8,9},{9,10},{10,11},{12,13},{... | collective-permute-start | bytes 207368 | tf_op jit(solution)/shard_map/ppermute | solution.py:19
  50.8 1.6 collective-permute-done.7
  53.6 1.3 collective-permute-start.8
  54.9 4.9 %collective-permute-start.9 = (f32[4,3,1,1440]{3,2,1,0:T(1,128)S(1)}, f32[4,3,1,1440]{3,2,1,0:T(1,128)S(1)}, u32[]{:S(2)}, u32[]{:S(2)}) collective-permute-start(f32[4,3,1,1440]{3,2,1,0:T(1,128)S(1)} %get-tuple-element.179), channel_id=1, source_target_pairs={{0,1},{1,2},{2,3},{4,5},{5,6},{6,7},{8,9},{9,10},{10,11},{12,13},{... | collective-permute-start | bytes 207368 | tf_op jit(solution)/shard_map/ppermute | solution.py:19
  60.2 1.6 collective-permute-done.9
  63.1 1.3 collective-permute-start.10
  64.4 5.1 %collective-permute-start.11 = (f32[4,3,1,1440]{3,2,1,0:T(1,128)S(1)}, f32[4,3,1,1440]{3,2,1,0:T(1,128)S(1)}, u32[]{:S(2)}, u32[]{:S(2)}) collective-permute-start(f32[4,3,1,1440]{3,2,1,0:T(1,128)S(1)} %get-tuple-element.173), channel_id=1, source_target_pairs={{0,1},{1,2},{2,3},{4,5},{5,6},{6,7},{8,9},{9,10},{10,11},{12,13},{... | collective-permute-start | bytes 207368 | tf_op jit(solution)/shard_map/ppermute | solution.py:19
  69.7 1.6 collective-permute-done.11
  72.5 1.3 collective-permute-start.12
  73.8 4.9 %collective-permute-start.13 = (f32[4,3,1,1440]{3,2,1,0:T(1,128)S(1)}, f32[4,3,1,1440]{3,2,1,0:T(1,128)S(1)}, u32[]{:S(2)}, u32[]{:S(2)}) collective-permute-start(f32[4,3,1,1440]{3,2,1,0:T(1,128)S(1)} %get-tuple-element.167), channel_id=1, source_target_pairs={{0,1},{1,2},{2,3},{4,5},{5,6},{6,7},{8,9},{9,10},{10,11},{12,13},{... | collective-permute-start | bytes 207368 | tf_op jit(solution)/shard_map/ppermute | solution.py:19
  79.1 1.6 collective-permute-done.13
  82.0 1.3 collective-permute-start.14
  83.3 4.9 %collective-permute-start.15 = (f32[4,3,1,1440]{3,2,1,0:T(1,128)S(1)}, f32[4,3,1,1440]{3,2,1,0:T(1,128)S(1)}, u32[]{:S(2)}, u32[]{:S(2)}) collective-permute-start(f32[4,3,1,1440]{3,2,1,0:T(1,128)S(1)} %get-tuple-element.161), channel_id=1, source_target_pairs={{0,1},{1,2},{2,3},{4,5},{5,6},{6,7},{8,9},{9,10},{10,11},{12,13},{... | collective-permute-start | bytes 207368 | tf_op jit(solution)/shard_map/ppermute | solution.py:19
  88.6 1.6 collective-permute-done.15
  91.4 2.6 conditional.1
  92.7 1.4 fusion
  98.2 18.0 %all-gather.11.cloned.1.call-done = f32[4,4,17280]{2,1,0:T(4,128)} async-done(((f32[1,4,17280]{2,1,0:T(4,128)}), f32[4,4,17280]{2,1,0:T(4,128)}) %all-gather.11.cloned.1.call-update) | async-done | bytes 1105936 | tf_op jit(solution)/shard_map/all_gather | solution.py:29
  116.3 1.5 reduce_sum.46
  119.1 11.7 %psum.56 = f32[4,4]{0,1:T(4,128)S(1)} all-reduce(f32[4,4]{0,1:T(4,128)S(1)} %fusion.112), channel_id=1, replica_groups=mesh['member'=2,'vec'=4,'band'=4] {'band'}, use_global_device_ids=true, to_apply=%region_4.5 | all-reduce | flops 16 | bytes 128 | tf_op jit(solution)/shard_map/psum | solution.py:110
  133.6 1.3 fusion.113
  134.9 8.4 %psum.57 = f32[4,4]{0,1:T(4,128)S(1)} all-reduce(f32[4,4]{0,1:T(4,128)S(1)} %fusion.113), channel_id=1, replica_groups=mesh['member'=2,'vec'=4,'band'=4] {'band'}, use_global_device_ids=true, to_apply=%region_7.10 | all-reduce | flops 16 | bytes 128 | tf_op jit(solution)/shard_map/psum | solution.py:113
  146.8 14.0 %all-gather.13.cloned.1.call-done = f32[4,4,17280]{2,1,0:T(4,128)} async-done(((f32[1,4,17280]{2,1,0:T(4,128)}), f32[4,4,17280]{2,1,0:T(4,128)}) %all-gather.13.cloned.1.call-update) | async-done | bytes 1105936 | tf_op jit(solution)/shard_map/all_gather | solution.py:29
  160.8 1.5 reduce_sum.47
  163.6 11.9 %psum.58 = f32[4,4]{0,1:T(4,128)S(1)} all-reduce(f32[4,4]{0,1:T(4,128)S(1)} %fusion.114), channel_id=1, replica_groups=mesh['member'=2,'vec'=4,'band'=4] {'band'}, use_global_device_ids=true, to_apply=%region_9.12 | all-reduce | flops 16 | bytes 128 | tf_op jit(solution)/shard_map/psum | solution.py:110
  178.3 1.3 fusion.115
  179.6 8.4 %psum.59 = f32[4,4]{0,1:T(4,128)S(1)} all-reduce(f32[4,4]{0,1:T(4,128)S(1)} %fusion.115), channel_id=1, replica_groups=mesh['member'=2,'vec'=4,'band'=4] {'band'}, use_global_device_ids=true, to_apply=%region_10.13 | all-reduce | flops 16 | bytes 128 | tf_op jit(solution)/shard_map/psum | solution.py:113
  191.5 13.9 %all-gather.15.cloned.1.call-done = f32[4,4,17280]{2,1,0:T(4,128)} async-done(((f32[1,4,17280]{2,1,0:T(4,128)}), f32[4,4,17280]{2,1,0:T(4,128)}) %all-gather.15.cloned.1.call-update) | async-done | bytes 1105936 | tf_op jit(solution)/shard_map/all_gather | solution.py:29
  205.5 1.5 reduce_sum.48
  208.3 11.7 %psum.60 = f32[4,4]{0,1:T(4,128)S(1)} all-reduce(f32[4,4]{0,1:T(4,128)S(1)} %fusion.116), channel_id=1, replica_groups=mesh['member'=2,'vec'=4,'band'=4] {'band'}, use_global_device_ids=true, to_apply=%region_12.15 | all-reduce | flops 16 | bytes 128 | tf_op jit(solution)/shard_map/psum | solution.py:110
  222.8 1.3 fusion.117
  224.1 8.4 %psum.61 = f32[4,4]{0,1:T(4,128)S(1)} all-reduce(f32[4,4]{0,1:T(4,128)S(1)} %fusion.117), channel_id=1, replica_groups=mesh['member'=2,'vec'=4,'band'=4] {'band'}, use_global_device_ids=true, to_apply=%region_13.16 | all-reduce | flops 16 | bytes 128 | tf_op jit(solution)/shard_map/psum | solution.py:113
  237.3 12.7 %all-gather.17.cloned.1.call-done = f32[4,4,17280]{2,1,0:T(4,128)} async-done(((f32[1,4,17280]{2,1,0:T(4,128)}), f32[4,4,17280]{2,1,0:T(4,128)}) %all-gather.17.cloned.1.call-update) | async-done | bytes 1105936 | tf_op jit(solution)/shard_map/all_gather | solution.py:29
  250.0 1.5 reduce_sum.49
  252.8 11.7 %psum.62 = f32[4,4]{0,1:T(4,128)S(1)} all-reduce(f32[4,4]{0,1:T(4,128)S(1)} %fusion.118), channel_id=1, replica_groups=mesh['member'=2,'vec'=4,'band'=4] {'band'}, use_global_device_ids=true, to_apply=%region_15.18 | all-reduce | flops 16 | bytes 128 | tf_op jit(solution)/shard_map/psum | solution.py:110
  268.0 1.3 fusion.119
  269.3 8.4 %psum.63 = f32[4,4]{0,1:T(4,128)S(1)} all-reduce(f32[4,4]{0,1:T(4,128)S(1)} %fusion.119), channel_id=1, replica_groups=mesh['member'=2,'vec'=4,'band'=4] {'band'}, use_global_device_ids=true, to_apply=%region_16.19 | all-reduce | flops 16 | bytes 128 | tf_op jit(solution)/shard_map/psum | solution.py:113
  (142 shorter events, 44.7 us)
Async XLA Ops:
  7.2 10.8 %copy-start = (f32[4,3,4,1440]{3,2,1,0:T(4,128)S(1)}, f32[4,3,4,1440]{3,2,1,0:T(4,128)}, u32[]{:S(2)}) copy-start(f32[4,3,4,1440]{3,2,1,0:T(4,128)} %param.9) | copy-start | bytes 829444
  7.2 10.9 %copy-start.1 = (f32[4,4,1440]{2,1,0:T(4,128)S(1)}, f32[4,4,1440]{2,1,0:T(4,128)}, u32[]{:S(2)}) copy-start(f32[4,4,1440]{2,1,0:T(4,128)} %param.10) | copy-start | bytes 276484
  7.2 109.1 %all-gather.11.cloned.1.call-start = ((), (), s32[]{:S(2)}) async-start(), calls=%async_computation | async-start | bytes 1382400 | tf_op jit(solution)/shard_map/all_gather | solution.py:29
  9.1 14.1 %collective-permute-start = (f32[4,3,1,1440]{3,2,1,0:T(1,128)}, f32[4,3,1,1440]{3,2,1,0:T(1,128)S(1)}, u32[]{:S(2)}, u32[]{:S(2)}) collective-permute-start(f32[4,3,1,1440]{3,2,1,0:T(1,128)} %get-tuple-element.202), channel_id=1, source_target_pairs={{1,0},{2,1},{3,2},{5,4},{6,5},{7,6},{9,8},{10,9},{11,10},{13,12},{... | collective-permute-start | bytes 207368 | tf_op jit(solution)/shard_map/ppermute | solution.py:22
  10.4 12.8 %collective-permute-start.1 = (f32[4,3,1,1440]{3,2,1,0:T(1,128)}, f32[4,3,1,1440]{3,2,1,0:T(1,128)S(1)}, u32[]{:S(2)}, u32[]{:S(2)}) collective-permute-start(f32[4,3,1,1440]{3,2,1,0:T(1,128)} %get-tuple-element.203), channel_id=1, source_target_pairs={{0,1},{1,2},{2,3},{4,5},{5,6},{6,7},{8,9},{9,10},{10,11},{12,13},{... | collective-permute-start | bytes 207368 | tf_op jit(solution)/shard_map/ppermute | solution.py:19
  21.2 0.7 copy-start.4
  23.2 0.6 copy-start.2
  23.2 0.7 copy-start.3
  26.0 6.2 %collective-permute-start.2 = (f32[4,3,1,1440]{3,2,1,0:T(1,128)S(1)}, f32[4,3,1,1440]{3,2,1,0:T(1,128)S(1)}, u32[]{:S(2)}, u32[]{:S(2)}) collective-permute-start(f32[4,3,1,1440]{3,2,1,0:T(1,128)S(1)} %get-tuple-element.196), channel_id=1, source_target_pairs={{1,0},{2,1},{3,2},{5,4},{6,5},{7,6},{9,8},{10,9},{11,10},{13,12},{... | collective-permute-start | bytes 207368 | tf_op jit(solution)/shard_map/ppermute | solution.py:22
  27.3 6.5 %collective-permute-start.3 = (f32[4,3,1,1440]{3,2,1,0:T(1,128)S(1)}, f32[4,3,1,1440]{3,2,1,0:T(1,128)S(1)}, u32[]{:S(2)}, u32[]{:S(2)}) collective-permute-start(f32[4,3,1,1440]{3,2,1,0:T(1,128)S(1)} %get-tuple-element.197), channel_id=1, source_target_pairs={{0,1},{1,2},{2,3},{4,5},{5,6},{6,7},{8,9},{9,10},{10,11},{12,13},{... | collective-permute-start | bytes 207368 | tf_op jit(solution)/shard_map/ppermute | solution.py:19
  34.9 6.6 %collective-permute-start.4 = (f32[4,3,1,1440]{3,2,1,0:T(1,128)S(1)}, f32[4,3,1,1440]{3,2,1,0:T(1,128)S(1)}, u32[]{:S(2)}, u32[]{:S(2)}) collective-permute-start(f32[4,3,1,1440]{3,2,1,0:T(1,128)S(1)} %get-tuple-element.190), channel_id=1, source_target_pairs={{1,0},{2,1},{3,2},{5,4},{6,5},{7,6},{9,8},{10,9},{11,10},{13,12},{... | collective-permute-start | bytes 207368 | tf_op jit(solution)/shard_map/ppermute | solution.py:22
  36.2 6.9 %collective-permute-start.5 = (f32[4,3,1,1440]{3,2,1,0:T(1,128)S(1)}, f32[4,3,1,1440]{3,2,1,0:T(1,128)S(1)}, u32[]{:S(2)}, u32[]{:S(2)}) collective-permute-start(f32[4,3,1,1440]{3,2,1,0:T(1,128)S(1)} %get-tuple-element.191), channel_id=1, source_target_pairs={{0,1},{1,2},{2,3},{4,5},{5,6},{6,7},{8,9},{9,10},{10,11},{12,13},{... | collective-permute-start | bytes 207368 | tf_op jit(solution)/shard_map/ppermute | solution.py:19
  44.2 6.6 %collective-permute-start.6 = (f32[4,3,1,1440]{3,2,1,0:T(1,128)S(1)}, f32[4,3,1,1440]{3,2,1,0:T(1,128)S(1)}, u32[]{:S(2)}, u32[]{:S(2)}) collective-permute-start(f32[4,3,1,1440]{3,2,1,0:T(1,128)S(1)} %get-tuple-element.184), channel_id=1, source_target_pairs={{1,0},{2,1},{3,2},{5,4},{6,5},{7,6},{9,8},{10,9},{11,10},{13,12},{... | collective-permute-start | bytes 207368 | tf_op jit(solution)/shard_map/ppermute | solution.py:22
  45.5 6.9 %collective-permute-start.7 = (f32[4,3,1,1440]{3,2,1,0:T(1,128)S(1)}, f32[4,3,1,1440]{3,2,1,0:T(1,128)S(1)}, u32[]{:S(2)}, u32[]{:S(2)}) collective-permute-start(f32[4,3,1,1440]{3,2,1,0:T(1,128)S(1)} %get-tuple-element.185), channel_id=1, source_target_pairs={{0,1},{1,2},{2,3},{4,5},{5,6},{6,7},{8,9},{9,10},{10,11},{12,13},{... | collective-permute-start | bytes 207368 | tf_op jit(solution)/shard_map/ppermute | solution.py:19
  53.6 6.6 %collective-permute-start.8 = (f32[4,3,1,1440]{3,2,1,0:T(1,128)S(1)}, f32[4,3,1,1440]{3,2,1,0:T(1,128)S(1)}, u32[]{:S(2)}, u32[]{:S(2)}) collective-permute-start(f32[4,3,1,1440]{3,2,1,0:T(1,128)S(1)} %get-tuple-element.178), channel_id=1, source_target_pairs={{1,0},{2,1},{3,2},{5,4},{6,5},{7,6},{9,8},{10,9},{11,10},{13,12},{... | collective-permute-start | bytes 207368 | tf_op jit(solution)/shard_map/ppermute | solution.py:22
  54.9 6.9 %collective-permute-start.9 = (f32[4,3,1,1440]{3,2,1,0:T(1,128)S(1)}, f32[4,3,1,1440]{3,2,1,0:T(1,128)S(1)}, u32[]{:S(2)}, u32[]{:S(2)}) collective-permute-start(f32[4,3,1,1440]{3,2,1,0:T(1,128)S(1)} %get-tuple-element.179), channel_id=1, source_target_pairs={{0,1},{1,2},{2,3},{4,5},{5,6},{6,7},{8,9},{9,10},{10,11},{12,13},{... | collective-permute-start | bytes 207368 | tf_op jit(solution)/shard_map/ppermute | solution.py:19
  63.1 6.6 %collective-permute-start.10 = (f32[4,3,1,1440]{3,2,1,0:T(1,128)S(1)}, f32[4,3,1,1440]{3,2,1,0:T(1,128)S(1)}, u32[]{:S(2)}, u32[]{:S(2)}) collective-permute-start(f32[4,3,1,1440]{3,2,1,0:T(1,128)S(1)} %get-tuple-element.172), channel_id=1, source_target_pairs={{1,0},{2,1},{3,2},{5,4},{6,5},{7,6},{9,8},{10,9},{11,10},{13,12},{... | collective-permute-start | bytes 207368 | tf_op jit(solution)/shard_map/ppermute | solution.py:22
  64.4 6.9 %collective-permute-start.11 = (f32[4,3,1,1440]{3,2,1,0:T(1,128)S(1)}, f32[4,3,1,1440]{3,2,1,0:T(1,128)S(1)}, u32[]{:S(2)}, u32[]{:S(2)}) collective-permute-start(f32[4,3,1,1440]{3,2,1,0:T(1,128)S(1)} %get-tuple-element.173), channel_id=1, source_target_pairs={{0,1},{1,2},{2,3},{4,5},{5,6},{6,7},{8,9},{9,10},{10,11},{12,13},{... | collective-permute-start | bytes 207368 | tf_op jit(solution)/shard_map/ppermute | solution.py:19
  72.5 6.6 %collective-permute-start.12 = (f32[4,3,1,1440]{3,2,1,0:T(1,128)S(1)}, f32[4,3,1,1440]{3,2,1,0:T(1,128)S(1)}, u32[]{:S(2)}, u32[]{:S(2)}) collective-permute-start(f32[4,3,1,1440]{3,2,1,0:T(1,128)S(1)} %get-tuple-element.166), channel_id=1, source_target_pairs={{1,0},{2,1},{3,2},{5,4},{6,5},{7,6},{9,8},{10,9},{11,10},{13,12},{... | collective-permute-start | bytes 207368 | tf_op jit(solution)/shard_map/ppermute | solution.py:22
  73.8 6.9 %collective-permute-start.13 = (f32[4,3,1,1440]{3,2,1,0:T(1,128)S(1)}, f32[4,3,1,1440]{3,2,1,0:T(1,128)S(1)}, u32[]{:S(2)}, u32[]{:S(2)}) collective-permute-start(f32[4,3,1,1440]{3,2,1,0:T(1,128)S(1)} %get-tuple-element.167), channel_id=1, source_target_pairs={{0,1},{1,2},{2,3},{4,5},{5,6},{6,7},{8,9},{9,10},{10,11},{12,13},{... | collective-permute-start | bytes 207368 | tf_op jit(solution)/shard_map/ppermute | solution.py:19
  82.0 6.6 %collective-permute-start.14 = (f32[4,3,1,1440]{3,2,1,0:T(1,128)S(1)}, f32[4,3,1,1440]{3,2,1,0:T(1,128)S(1)}, u32[]{:S(2)}, u32[]{:S(2)}) collective-permute-start(f32[4,3,1,1440]{3,2,1,0:T(1,128)S(1)} %get-tuple-element.160), channel_id=1, source_target_pairs={{1,0},{2,1},{3,2},{5,4},{6,5},{7,6},{9,8},{10,9},{11,10},{13,12},{... | collective-permute-start | bytes 207368 | tf_op jit(solution)/shard_map/ppermute | solution.py:22
  83.3 6.9 %collective-permute-start.15 = (f32[4,3,1,1440]{3,2,1,0:T(1,128)S(1)}, f32[4,3,1,1440]{3,2,1,0:T(1,128)S(1)}, u32[]{:S(2)}, u32[]{:S(2)}) collective-permute-start(f32[4,3,1,1440]{3,2,1,0:T(1,128)S(1)} %get-tuple-element.161), channel_id=1, source_target_pairs={{0,1},{1,2},{2,3},{4,5},{5,6},{6,7},{8,9},{9,10},{10,11},{12,13},{... | collective-permute-start | bytes 207368 | tf_op jit(solution)/shard_map/ppermute | solution.py:19
  90.8 0.7 copy-start.5
  95.3 65.5 %all-gather.13.cloned.1.call-start = ((), (), s32[]{:S(2)}) async-start(), calls=%async_computation.1 | async-start | bytes 1382400 | tf_op jit(solution)/shard_map/all_gather | solution.py:29
  144.9 60.6 %all-gather.15.cloned.1.call-start = ((), (), s32[]{:S(2)}) async-start(), calls=%async_computation.2 | async-start | bytes 1382400 | tf_op jit(solution)/shard_map/all_gather | solution.py:29
  189.6 60.4 %all-gather.17.cloned.1.call-start = ((), (), s32[]{:S(2)}) async-start(), calls=%async_computation.3 | async-start | bytes 1382400 | tf_op jit(solution)/shard_map/all_gather | solution.py:29
Sparse Core Ops, SparseCore 0:
  95.4 20.8 all-gather.10
  145.0 15.7 all-gather.12
  189.7 15.7 all-gather.14
  234.2 15.7 all-gather.16
